TPU v7x, 256 devices: a whole 4x4x8 slice. The times are simulated.
256 devices in a mesh: row: 32 (over z, x), col: 8 (over y, core).
Axes of the slice: x: 4, y: 4, z: 8, core: 2. Of those that a mesh axis runs over, the one named last changes fastest.
Arguments:
- right_side: float32 [15, 512, 512], P(None, 'row'), may hold values from -6 to 6
- off_blocks: float32 [8, 512, 2176], P('col', 'row'), may hold values from -0.09375 to 0.09375
- diag_inverse: float32 [8, 512, 960], P('col', 'row'), as said below
Outputs:
- forward_solution: float32 [8, 960, 512], P('col')
- solution: float32 [8, 4, 512, 512], P('col', None, 'row')
Inputs may be any that keep to these rules, and one draw needn't show every extreme that they name: `diag_inverse`: read through the block map of the first step, each block D(n) is lower triangular with a positive diagonal between 0.5 and 2.
All inputs are finite; a program needn't handle non-finite values.
Results may differ from a plain program's by a relative error of at most 0.00011.
Values sent between devices are 32-bit elements; how exact they have to be, the bound alone decides.
No kernel may reach another device: no remote copies, remote signals or barrier semaphores. Data moves between devices by JAX's collectives and lax.ppermute only.
A program may use at most 64 MiB of HBM per device.

v0:
```python
import jax
import jax.numpy as jnp
from jax import lax
from jax.sharding import PartitionSpec as P

W = 512
LEVELS = 4


def swapped(value, axis, apart):
    mask = 2**apart
    pairs = [(source, source ^ mask) for source in range(lax.axis_size(axis))]
    return lax.ppermute(value, axis, pairs)


def pair_start(depth_down, depth_up):
    return (depth_down - 2) * 2**depth_down + 2 + depth_up * 2**depth_down


def group_sum(values, bit_count):
    for bit_num in range(bit_count):
        values = values + swapped(values, "col", bit_num)
    return values


def solve_block(right_side, off_blocks, diag_inverse):
    highest = lax.Precision.HIGHEST
    col_count = lax.axis_size("col")
    column = lax.axis_index("col")
    totals = [None] * LEVELS
    forward = [None] * LEVELS
    for depth_now in reversed(range(LEVELS)):
        group = col_count >> depth_now
        width = W // group
        bit_count = group.bit_length() - 1
        node_index = 2**depth_now - 1 + column // group
        residue = lax.dynamic_index_in_dim(right_side, node_index, 0, keepdims=False)
        if totals[depth_now] is not None:
            residue = residue - group_sum(totals[depth_now], bit_count)
        start = (2**depth_now - 1) * W // col_count
        inverse = diag_inverse[0, :, start : start + width]
        partial_value = jnp.einsum(
            "ba,br->ar", inverse, residue, precision=highest, preferred_element_type=jnp.float32
        )
        solved = lax.psum(partial_value, "row")
        forward[depth_now] = solved
        for depth_up in range(depth_now):
            begin = pair_start(depth_now, depth_up) * W // col_count
            block = off_blocks[0, :, begin : begin + width]
            term = jnp.dot(block, solved, precision=highest, preferred_element_type=jnp.float32)
            totals[depth_up] = term if totals[depth_up] is None else totals[depth_up] + term
    totals_down = [None] * LEVELS
    backward = [None] * LEVELS
    for depth_now in range(LEVELS):
        group = col_count >> depth_now
        width = W // group
        bit_count = group.bit_length() - 1
        residue = forward[depth_now]
        if totals_down[depth_now] is not None:
            residue = residue - lax.psum(totals_down[depth_now], "row")
        start = (2**depth_now - 1) * W // col_count
        inverse = diag_inverse[0, :, start : start + width]
        partial_value = jnp.dot(
            inverse, residue, precision=highest, preferred_element_type=jnp.float32
        )
        solved = group_sum(partial_value, bit_count)
        backward[depth_now] = solved
        for depth_down in range(depth_now + 1, LEVELS):
            width_down = W // (col_count >> depth_down)
            begin = pair_start(depth_down, depth_now) * W // col_count
            block = off_blocks[0, :, begin : begin + width_down]
            term = jnp.einsum(
                "ij,ir->jr", block, solved, precision=highest, preferred_element_type=jnp.float32
            )
            totals_down[depth_down] = (
                term if totals_down[depth_down] is None else totals_down[depth_down] + term
            )
    return (jnp.concatenate(forward, axis=0)[None], jnp.stack(backward, axis=0)[None])


def per_device(right_side, off_blocks, diag_inverse):
    forward_piece, backward_piece = solve_block(right_side, off_blocks, diag_inverse)
    return (forward_piece, backward_piece)


def solution(mesh):
    return jax.shard_map(
        per_device,
        mesh=mesh,
        in_specs=(P(None, "row", None), P("col", "row", None), P("col", "row", None)),
        out_specs=(P("col", None, None), P("col", None, "row", None)),
        check_vma=False,
    )
```

profile of v0, /device:TPU:8, one launch (start us, length us, event | category | flops | bytes accessed | tf_op | source)
XLA Modules:
  0.0 1091.3 jit_solution(8329834675328494492)
XLA Ops:
  7.2 2.9 convolution_bitcast_fusion
  10.2 154.2 %all-reduce.8.cloned.1.call-done = f32[512,512]{0,1:T(8,128)} async-done(((f32[512,512]{0,1:T(8,128)}), f32[512,512]{0,1:T(8,128)}) %all-reduce.8.cloned.1.call-update) | async-done | bytes 1048592 | tf_op jit(solution)/shard_map/psum | solution.py:45
  164.3 2.3 convolution_bitcast_fusion.8
  166.7 1.2 collective-permute-done
  167.9 2.2 convolution_bitcast_fusion.1
  170.2 144.9 %all-reduce.10.cloned.1.call-done = f32[256,512]{0,1:T(8,128)} async-done(((f32[256,512]{0,1:T(8,128)}), f32[256,512]{0,1:T(8,128)}) %all-reduce.10.cloned.1.call-update) | async-done | bytes 524304 | tf_op jit(solution)/shard_map/psum | solution.py:45
  315.1 1.7 fusion.36
  316.8 1.0 fusion.4
  317.8 1.2 collective-permute-done.1
  319.0 0.5 collective-permute-start.2
  319.6 3.4 collective-permute-done.2
  323.0 2.1 convolution_bitcast_fusion.4
  325.1 0.5 fusion.39
  325.7 1.0 convolution_add_fusion.4
  326.7 139.5 %all-reduce.12.cloned.1.call-done = f32[128,512]{0,1:T(8,128)} async-done(((f32[128,512]{0,1:T(8,128)}), f32[128,512]{0,1:T(8,128)}) %all-reduce.12.cloned.1.call-update) | async-done | bytes 262160 | tf_op jit(solution)/shard_map/psum | solution.py:45
  466.2 1.4 fusion.3
  467.6 1.2 collective-permute-done.3
  468.8 0.5 collective-permute-start.4
  469.4 3.4 collective-permute-done.4
  472.8 2.1 collective-permute-start.5
  474.9 3.3 collective-permute-done.5
  478.2 2.1 convolution_bitcast_fusion.3
  480.3 141.1 %all-reduce.14.cloned.1.call-done = f32[64,512]{0,1:T(8,128)} async-done(((f32[64,512]{0,1:T(8,128)}), f32[64,512]{0,1:T(8,128)}) %all-reduce.14.cloned.1.call-update) | async-done | bytes 131088 | tf_op jit(solution)/shard_map/psum | solution.py:45
  621.5 1.3 convolution_bitcast_fusion.7
  622.8 1.2 collective-permute-done.6
  624.0 0.5 collective-permute-start.7
  624.6 3.4 collective-permute-done.7
  628.0 2.1 collective-permute-start.8
  630.1 3.3 collective-permute-done.8
  633.4 1.3 convolution_bitcast_fusion.2
  634.7 0.2 all-reduce.18.cloned.1.call-start
  634.9 141.0 %all-reduce.16.cloned.1.call-done = f32[128,512]{0,1:T(8,128)} async-done(((f32[128,512]{0,1:T(8,128)}), f32[128,512]{0,1:T(8,128)}) %all-reduce.16.cloned.1.call-update) | async-done | bytes 262160 | tf_op jit(solution)/shard_map/psum | solution.py:60
  775.9 1.3 convolution_bitcast_fusion.6
  777.3 1.2 collective-permute-done.9
  778.5 0.5 collective-permute-start.10
  779.0 3.4 collective-permute-done.10
  782.4 0.6 fusion.34
  783.0 1.4 fusion.2
  784.5 144.5 %all-reduce.18.cloned.1.call-done = f32[256,512]{0,1:T(8,128)} async-done(((f32[256,512]{0,1:T(8,128)}), f32[256,512]{0,1:T(8,128)}) %all-reduce.18.cloned.1.call-update) | async-done | bytes 524304 | tf_op jit(solution)/shard_map/psum | solution.py:60
  929.0 1.6 convolution_bitcast_fusion.9
  930.7 1.0 fusion.8
  931.9 1.0 fusion.11
  932.9 2.0 fusion.1
  935.0 1.8 maximum_bitcast_fusion
  936.9 1.8 copy.6
  938.7 142.9 %all-reduce.20.cloned.1.call-done = f32[512,512]{0,1:T(8,128)} async-done(((f32[512,512]{0,1:T(8,128)}), f32[512,512]{0,1:T(8,128)}) %all-reduce.20.cloned.1.call-update) | async-done | bytes 1048592 | tf_op jit(solution)/shard_map/psum | solution.py:60
  1081.6 2.2 convolution_bitcast_fusion.5
  1083.8 0.7 maximum_bitcast_fusion.1
  (45 shorter events, 1.1 us)
Async XLA Ops:
  7.2 160.7 %copy-start.4 = (f32[1,16,960]{2,1,0:T(8,128)S(1)}, f32[1,16,960]{2,1,0:T(8,128)}, u32[]{:S(2)}) copy-start(f32[1,16,960]{2,1,0:T(8,128)} %param.5) | copy-start | bytes 184324
  7.2 157.2 %copy-start.3 = (f32[1,16,2176]{2,1,0:T(8,128)S(1)}, f32[1,16,2176]{2,1,0:T(8,128)}, u32[]{:S(2)}) copy-start(f32[1,16,2176]{2,1,0:T(8,128)} %param.4) | copy-start | bytes 417796
  7.2 157.1 %all-reduce.8.cloned.1.call-start = ((), (), s32[]{:S(2)}) async-start(), calls=%async_computation | async-start | bytes 2097152 | tf_op jit(solution)/shard_map/psum | solution.py:45
  10.1 305.0 %all-reduce.10.cloned.1.call-start = ((), (), s32[]{:S(2)}) async-start(), calls=%async_computation.1 | async-start | bytes 1048576 | tf_op jit(solution)/shard_map/psum | solution.py:45
  164.3 152.4 %copy-start = (f32[512,512]{0,1:T(8,128)S(1)}, f32[512,512]{0,1:T(8,128)}, u32[]{:S(2)}) copy-start(f32[512,512]{0,1:T(8,128)} %all-reduce.8.cloned.1.call-done) | copy-start | bytes 3145732
  166.6 1.3 collective-permute-start
  170.1 296.1 %all-reduce.12.cloned.1.call-start = ((), (), s32[]{:S(2)}) async-start(), calls=%async_computation.2 | async-start | bytes 524288 | tf_op jit(solution)/shard_map/psum | solution.py:45
  315.1 10.0 copy-start.1
  317.8 1.3 collective-permute-start.1
  319.0 3.9 collective-permute-start.2
  325.1 296.4 %all-reduce.14.cloned.1.call-start = ((), (), s32[]{:S(2)}) async-start(), calls=%async_computation.3 | async-start | bytes 524288 | tf_op jit(solution)/shard_map/psum | solution.py:45
  466.2 309.7 %copy-start.2 = (f32[128,512]{0,1:T(8,128)S(1)}, f32[128,512]{0,1:T(8,128)}, u32[]{:S(2)}) copy-start(f32[128,512]{0,1:T(8,128)} %all-reduce.12.cloned.1.call-done) | copy-start | bytes 786436
  467.5 1.3 collective-permute-start.3
  468.8 3.9 collective-permute-start.4
  472.8 5.4 collective-permute-start.5
  480.3 295.6 %all-reduce.16.cloned.1.call-start = ((), (), s32[]{:S(2)}) async-start(), calls=%async_computation.4 | async-start | bytes 524288 | tf_op jit(solution)/shard_map/psum | solution.py:60
  622.7 1.3 collective-permute-start.6
  624.0 3.9 collective-permute-start.7
  628.0 5.4 collective-permute-start.8
  634.7 294.3 %all-reduce.18.cloned.1.call-start = ((), (), s32[]{:S(2)}) async-start(), calls=%async_computation.5 | async-start | bytes 1048576 | tf_op jit(solution)/shard_map/psum | solution.py:60
  777.2 1.3 collective-permute-start.9
  778.5 3.9 collective-permute-start.10
  784.5 297.1 %all-reduce.20.cloned.1.call-start = ((), (), s32[]{:S(2)}) async-start(), calls=%async_computation.6 | async-start | bytes 2097152 | tf_op jit(solution)/shard_map/psum | solution.py:60
  930.6 1.3 collective-permute-start.11
  931.9 3.1 copy-start.6
  936.9 1.8 copy-start.7
  936.9 144.7 %copy-start.5 = (f32[1,16,960]{2,1,0:T(8,128)S(1)}, f32[1,16,960]{2,1,0:T(8,128)}, u32[]{:S(2)}) copy-start(f32[1,16,960]{2,1,0:T(8,128)} %param.5) | copy-start | bytes 184324
Sparse Core Ops, SparseCore 0:
  12.0 152.2 all-reduce.7
  170.2 144.8 all-reduce.9
  325.2 140.9 all-reduce.11
  480.4 141.0 all-reduce.13
  634.8 141.0 all-reduce.15
  784.6 144.4 all-reduce.17
  935.1 146.3 all-reduce.19
where the time goes:
time: 1090 us
  waiting for transfers between devices  1030 us (94%)
  matrix products  30.9 us (3%)
  between operations  14.3 us (1%)
    psum x4, waiting for transfers between devices, solve_block(): solved = lax.psum(partial_value, 'row')  580 us
    psum x3, waiting for transfers between devices, solve_block(): residue = residue - lax.psum(totals_down[depth_now], 'row')  428 us
    ppermute x12, waiting for transfers between devices, swapped(): return lax.ppermute(value, axis, pairs)  26.2 us
  transfers between devices with their start and end apart: 19, of which 19 were waited for; matrix products, arithmetic and copies ran while one was open for 1% of the time, Pallas kernels for 0%

commit v1 on v0

--- a/solution.py
+++ b/solution.py
@@ -42,7 +42,11 @@
         partial_value = jnp.einsum(
             "ba,br->ar", inverse, residue, precision=highest, preferred_element_type=jnp.float32
         )
-        solved = lax.psum(partial_value, "row")
+
+        def _refer_rows(incoming_x, lane_axis):
+            return jnp.sum(lax.all_gather(incoming_x, lane_axis), axis=0)
+
+        solved = _refer_rows(partial_value, "row")
         forward[depth_now] = solved
         for depth_up in range(depth_now):
             begin = pair_start(depth_now, depth_up) * W // col_count

time: 1090 us -> 1140 us (1.046)
  local copies, waits for them, and re-layouts: 1.8 us -> 56.5 us
  other arithmetic: 2.59 us -> 20.9 us
    psum x4 -> x0, waiting for transfers between devices: 580 us -> none  [solve_block(): solved = lax.psum(partial_value, 'row')]
    all_gather x0 -> x4, waiting for transfers between devices: none -> 563 us  [_refer_rows(): return jnp.sum(lax.all_gather(incoming_x, lane_axis), axis=0)]
    unnamed x17 -> x8, local copies, waits for them, and re-layouts: 1.8 us -> 56.4 us
    reduce_sum x0 -> x4, other arithmetic: none -> 18.1 us  [_refer_rows(): return jnp.sum(lax.all_gather(incoming_x, lane_axis), axis=0)]
where the time goes in v1:
time: 1140 us
  waiting for transfers between devices  1020 us (89%)
  local copies, waits for them, and re-layouts  56.5 us (5%)
  matrix products  26 us (2%)
  other arithmetic  20.9 us (2%)
  between operations  14.3 us (1%)
    all_gather x4, waiting for transfers between devices, _refer_rows(): return jnp.sum(lax.all_gather(incoming_x, lane_axis), axis=0)  563 us
    psum x3, waiting for transfers between devices, solve_block(): residue = residue - lax.psum(totals_down[depth_now], 'row')  427 us
    unnamed x8, local copies, waits for them, and re-layouts  56.4 us
    ppermute x12, waiting for transfers between devices, swapped(): return lax.ppermute(value, axis, pairs)  26.2 us
  transfers between devices with their start and end apart: 19, of which 19 were waited for; matrix products, arithmetic and copies ran while one was open for 1% of the time, Pallas kernels for 0%

profile of v1, /device:TPU:8, one launch (start us, length us, event | category | flops | bytes accessed | tf_op | source)
XLA Modules:
  0.0 1142.2 jit_solution(16321631131346330411)
XLA Ops:
  7.2 2.8 convolution_bitcast_fusion
  10.1 237.2 %all-gather.9.cloned.1.call-done = f32[16384,512]{0,1:T(8,128)} async-done(((f32[512,512]{0,1:T(8,128)}), f32[16384,512]{0,1:T(8,128)}) %all-gather.9.cloned.1.call-update) | async-done | bytes 33554448 | tf_op jit(solution)/shard_map/all_gather | solution.py:47
  247.3 32.5 %copy.8 = f32[64,8,32,512]{3,2,1,0:T(8,128)S(1)} copy(f32[64,8,32,512]{3,1,2,0:T(8,128)} %bitcast.127) | data formatting | bytes 67108864
  279.9 5.4 bitcast_reduce_fusion
  285.2 1.0 convolution_bitcast_fusion.8
  286.3 1.2 collective-permute-done
  287.5 2.2 convolution_bitcast_fusion.1
  289.9 147.7 %all-gather.11.cloned.1.call-done = f32[8192,512]{0,1:T(8,128)} async-done(((f32[256,512]{0,1:T(8,128)}), f32[8192,512]{0,1:T(8,128)}) %all-gather.11.cloned.1.call-update) | async-done | bytes 16777232 | tf_op jit(solution)/shard_map/all_gather | solution.py:47
  437.6 15.8 %copy.9 = f32[64,8,32,256]{3,2,1,0:T(8,128)} copy(f32[64,8,32,256]{3,1,2,0:T(8,128)} %bitcast.128) | data formatting | bytes 33554432
  453.4 8.7 bitcast_reduce_fusion.1
  462.1 0.5 fusion.36
  462.6 1.0 fusion.4
  463.7 1.2 collective-permute-done.1
  465.4 3.4 collective-permute-done.2
  468.8 2.1 convolution_bitcast_fusion.3
  471.2 0.5 fusion.39
  471.7 1.0 convolution_add_fusion.4
  472.7 98.8 %all-gather.13.cloned.1.call-done = f32[4096,512]{0,1:T(8,128)} async-done(((f32[128,512]{0,1:T(8,128)}), f32[4096,512]{0,1:T(8,128)}) %all-gather.13.cloned.1.call-update) | async-done | bytes 8388624 | tf_op jit(solution)/shard_map/all_gather | solution.py:47
  571.6 5.2 copy.10
  576.8 1.6 bitcast_reduce_fusion.2
  578.8 1.2 collective-permute-done.3
  580.5 3.4 collective-permute-done.4
  583.9 2.1 collective-permute-start.5
  586.0 3.3 collective-permute-done.5
  589.3 1.7 convolution_bitcast_fusion.4
  591.1 79.5 %all-gather.15.cloned.1.call-done = f32[2048,512]{1,0:T(8,128)} async-done(((f32[64,512]{1,0:T(8,128)}), f32[2048,512]{1,0:T(8,128)}) %all-gather.15.cloned.1.call-update) | async-done | bytes 4194320 | tf_op jit(solution)/shard_map/all_gather | solution.py:47
  670.6 2.5 reduce_sum.39
  673.4 1.2 collective-permute-done.6
  675.2 3.4 collective-permute-done.7
  678.6 2.1 collective-permute-start.8
  680.7 3.3 collective-permute-done.8
  684.0 1.3 convolution_bitcast_fusion.2
  685.4 141.4 %all-reduce.4.cloned.1.call-done = f32[128,512]{0,1:T(8,128)} async-done(((f32[128,512]{0,1:T(8,128)}), f32[128,512]{0,1:T(8,128)}) %all-reduce.4.cloned.1.call-update) | async-done | bytes 262160 | tf_op jit(solution)/shard_map/psum | solution.py:64
  826.8 1.3 convolution_bitcast_fusion.6
  828.2 1.2 collective-permute-done.9
  829.9 3.4 collective-permute-done.10
  833.3 0.6 fusion.34
  833.9 1.4 fusion.2
  835.7 144.2 %all-reduce.6.cloned.1.call-done = f32[256,512]{0,1:T(8,128)} async-done(((f32[256,512]{0,1:T(8,128)}), f32[256,512]{0,1:T(8,128)}) %all-reduce.6.cloned.1.call-update) | async-done | bytes 524304 | tf_op jit(solution)/shard_map/psum | solution.py:64
  979.9 1.6 convolution_bitcast_fusion.9
  981.6 1.0 fusion.8
  982.8 1.0 fusion.11
  983.8 2.0 fusion.1
  986.0 2.1 maximum_bitcast_fusion
  988.1 2.8 copy.7
  990.9 141.5 %all-reduce.8.cloned.1.call-done = f32[512,512]{0,1:T(8,128)} async-done(((f32[512,512]{0,1:T(8,128)}), f32[512,512]{0,1:T(8,128)}) %all-reduce.8.cloned.1.call-update) | async-done | bytes 1048592 | tf_op jit(solution)/shard_map/psum | solution.py:64
  1132.4 2.2 convolution_bitcast_fusion.5
  1134.7 0.7 maximum_bitcast_fusion.1
  (41 shorter events, 4.5 us)
Async XLA Ops:
  7.2 240.2 %all-gather.9.cloned.1.call-start = ((), (), s32[]{:S(2)}) async-start(), calls=%async_computation.3 | async-start | bytes 34603008 | tf_op jit(solution)/shard_map/all_gather | solution.py:47
  10.1 427.5 %all-gather.11.cloned.1.call-start = ((), (), s32[]{:S(2)}) async-start(), calls=%async_computation.4 | async-start | bytes 17301504 | tf_op jit(solution)/shard_map/all_gather | solution.py:47
  279.8 5.4 copy-start
  279.8 7.6 copy-start.1
  286.2 1.2 collective-permute-start
  289.7 281.9 %all-gather.13.cloned.1.call-start = ((), (), s32[]{:S(2)}) async-start(), calls=%async_computation.5 | async-start | bytes 8650752 | tf_op jit(solution)/shard_map/all_gather | solution.py:47
  463.6 1.3 collective-permute-start.1
  464.9 3.9 collective-permute-start.2
  470.9 199.7 %all-gather.15.cloned.1.call-start = ((), (), s32[]{:S(2)}) async-start(), calls=%async_computation.6 | async-start | bytes 4325376 | tf_op jit(solution)/shard_map/all_gather | solution.py:47
  578.7 1.3 collective-permute-start.3
  580.0 3.9 collective-permute-start.4
  583.9 5.4 collective-permute-start.5
  591.1 235.7 %all-reduce.4.cloned.1.call-start = ((), (), s32[]{:S(2)}) async-start(), calls=%async_computation | async-start | bytes 524288 | tf_op jit(solution)/shard_map/psum | solution.py:64
  673.3 1.3 collective-permute-start.6
  674.6 3.9 collective-permute-start.7
  678.6 5.4 collective-permute-start.8
  685.3 294.6 %all-reduce.6.cloned.1.call-start = ((), (), s32[]{:S(2)}) async-start(), calls=%async_computation.1 | async-start | bytes 1048576 | tf_op jit(solution)/shard_map/psum | solution.py:64
  828.1 1.3 collective-permute-start.9
  829.4 3.9 collective-permute-start.10
  835.4 297.1 %all-reduce.8.cloned.1.call-start = ((), (), s32[]{:S(2)}) async-start(), calls=%async_computation.2 | async-start | bytes 2097152 | tf_op jit(solution)/shard_map/psum | solution.py:64
  981.5 1.3 collective-permute-start.11
Sparse Core Ops, SparseCore 0:
  11.2 236.1 all-gather.8
  289.8 147.7 all-gather.10
  471.0 100.4 all-gather.12
  591.2 79.3 all-gather.14
  685.4 141.3 all-reduce.3
  835.5 144.3 all-reduce.5
  986.0 146.3 all-reduce.7
